TPU v7x, 32 devices: a whole 2x2x4 slice. The times are simulated.
32 devices in a mesh: ha: 8 (over z, core), wa: 4 (over y, x).
Axes of the slice: x: 2, y: 2, z: 4, core: 2. Of those that a mesh axis runs over, the one named last changes fastest.
Arguments:
- latents: bfloat16 [64, 64, 64, 512], P('ha', 'wa'), may hold values from -8 to 8
- cotangent: bfloat16 [64, 64, 64, 512], P('ha', 'wa'), may hold values from -0.59765625 to 0.59765625
- w_down: bfloat16 [512, 18], replicated, may hold values from -0.25 to 0.25
- bit_bias: float32 [18], replicated, may hold values from -1.5 to 1.5
- w_up: bfloat16 [18, 512], replicated, may hold values from -1.5 to 1.5
Outputs:
- grad_latents: bfloat16 [64, 64, 64, 512], P('ha', 'wa')
- bit_entropy: float32 [64, 64, 64], P('ha', 'wa')
- marginal: float32 [18], replicated
- grad_down: float32 [512, 18], replicated
- grad_bias: float32 [18], replicated
- grad_up: float32 [18, 512], replicated
All inputs are finite; a program needn't handle non-finite values.
Results may differ from a plain program's by a relative error of at most 0.005.
Values may be sent and summed in bfloat16 or wider, within the bound.
No kernel may reach another device: no remote copies, remote signals or barrier semaphores. Data moves between devices by JAX's collectives and lax.ppermute only.
A program may use at most 128 MiB of HBM per device.

v0:
```python
import jax
import jax.numpy as jnp
from jax import lax
from jax.sharding import PartitionSpec as P

local_weight = 4.0
margin_weight = 4.0


def extended_2(cells, sides, width):
    for axis, dim in sides:
        count = lax.axis_size(axis)
        head = lax.slice_in_dim(cells, 0, width, axis=dim)
        tail = lax.slice_in_dim(cells, cells.shape[dim] - width, cells.shape[dim], axis=dim)
        cells = jnp.concatenate(
            [
                lax.ppermute(tail, axis, [(i, (i + 1) % count) for i in range(count)]),
                cells,
                lax.ppermute(head, axis, [((i + 1) % count, i) for i in range(count)]),
            ],
            axis=dim,
        )
    return cells


def window(extended, rows, cols):
    total = extended[0:rows, 0:cols]
    for first in range(3):
        for second in range(3):
            if first or second:
                total = total + extended[first : first + rows, second : second + cols]
    return total / 9.0


def binary(values):
    return -values * jnp.log(values) - (1.0 - values) * jnp.log1p(-values)


def local(latents, cotangent, w_down, bit_bias, w_up):
    rows, cols, images, width = latents.shape
    bits = w_down.shape[1]
    count = rows * cols * images * lax.axis_size("ha") * lax.axis_size("wa")
    flattened = latents.reshape(-1, width)
    outward = cotangent.reshape(-1, width)
    layers = 1
    logits = jnp.dot(flattened, w_down, preferred_element_type=jnp.float32) + bit_bias
    squash = jax.nn.sigmoid(logits)
    prob = 0.01 + 0.98 * squash
    wide_prob = extended_2(prob.reshape(rows, cols, images, bits), (("ha", 0), ("wa", 1)), layers)
    local_mass = jnp.sum(prob, axis=0) / count
    marginal = lax.psum(local_mass, ("ha", "wa"))
    wide_pooled = window(wide_prob, rows + 2 * layers - 2, cols + 2 * layers - 2)
    slope = local_weight * jnp.log((1.0 - wide_pooled) / wide_pooled)
    wide_slope = extended_2(slope, (("ha", 0), ("wa", 1)), 1)
    bit_entropy = jnp.sum(binary(wide_pooled), axis=-1)
    code = (2.0 * squash - 1.0).astype(jnp.bfloat16)
    code_grad = jnp.dot(outward, w_up.T, preferred_element_type=jnp.float32)
    spread = window(wide_slope, rows, cols).reshape(-1, bits)
    steepness = squash * (1.0 - squash)
    base = ((2.0 * code_grad + 0.98 * spread) * steepness).astype(jnp.bfloat16)
    stacked = jnp.concatenate([base, steepness.astype(jnp.bfloat16)], axis=1)
    latent_part = (
        lax.dot_general(
            flattened, stacked, (((0,), (0,)), ((), ())), preferred_element_type=jnp.float32
        )
        / count
    )
    column_part = jnp.sum(stacked.astype(jnp.float32), axis=0) / count
    up_part = (
        lax.dot_general(code, outward, (((0,), (0,)), ((), ())), preferred_element_type=jnp.float32)
        / count
    )
    latent_total, column_total, grad_up = lax.psum(
        (latent_part, column_part, up_part), ("ha", "wa")
    )
    drift = margin_weight * jnp.log((1.0 - marginal) / marginal)
    logit_grad = ((2.0 * code_grad + 0.98 * (spread - drift)) * steepness).astype(jnp.bfloat16)
    grad_latents = jnp.dot(logit_grad, w_down.T, preferred_element_type=jnp.float32).astype(
        jnp.bfloat16
    )
    grad_latents = grad_latents.reshape(latents.shape)
    grad_down = latent_total[:, :bits] - 0.98 * drift * latent_total[:, bits:]
    grad_bias = column_total[:bits] - 0.98 * drift * column_total[bits:]
    return (grad_latents, bit_entropy, marginal, grad_down, grad_bias, grad_up)


def solution(mesh):
    placed = (P("ha", "wa", None, None), P("ha", "wa", None, None), P(), P(), P())
    return jax.shard_map(
        local,
        mesh=mesh,
        in_specs=placed,
        out_specs=(P("ha", "wa", None, None), P("ha", "wa", None), P(), P(), P(), P()),
        check_vma=False,
    )
```

profile of v0, /device:TPU:8, one launch (start us, length us, event | category | flops | bytes accessed | tf_op | source)
XLA Modules:
  0.0 191.5 jit_solution(5777653072572231376)
XLA Ops:
  7.2 0.0 copy-start
  7.2 0.0 all-reduce.3.cloned.1.call-start
  7.2 0.7 copy-done
  7.9 5.7 %multiply_add_fusion = (f32[8192,18]{0,1:T(8,128)S(1)}, f32[8192,18]{0,1:T(8,128)S(1)}) fusion(f32[18]{0:T(128)} %param.8, bf16[8192,512]{1,0:T(8,128)(2,1)} %bitcast.26, bf16[512,18]{0,1:T(8,128)(2,1)S(1)} %copy-done), kind=kOutput, calls=%fused_computation.59 | convolution fusion | flops 151879680 | bytes 9586760 | tf_op jit(solution)/shard_map/dot_general | solution.py:46
  13.6 0.1 slice.107
  13.7 0.0 collective-permute-start
  13.8 0.1 slice.109
  13.9 1.8 collective-permute-start.1
  15.6 0.5 reshape.34
  16.1 2.2 %collective-permute-done = f32[1,16,64,18]{2,1,0,3:T(8,128)S(1)} collective-permute-done((f32[1,16,64,18]{2,1,0,3:T(8,128)S(1)}, f32[1,16,64,18]{2,1,0,3:T(8,128)S(1)}, u32[]{:S(2)}, u32[]{:S(2)}) %collective-permute-start) | collective-permute-done | bytes 73760 | tf_op jit(solution)/shard_map/ppermute | solution.py:17
  18.3 0.1 constant_dynamic-update-slice_fusion.1
  18.4 0.7 collective-permute-done.1
  19.2 0.1 fusion.42
  19.3 2.0 %collective-permute-start.2 = (f32[10,1,64,18]{2,1,0,3:T(1,128)S(1)}, f32[10,1,64,18]{2,1,0,3:T(1,128)S(1)}, u32[]{:S(2)}, u32[]{:S(2)}) collective-permute-start(f32[10,1,64,18]{2,1,0,3:T(1,128)S(1)} %get-tuple-element.17), channel_id=1, source_target_pairs={{0,1},{1,2},{2,3},{3,0},{4,5},{5,6},{6,7},{7,4},{8,9},{9,10},{10,1... | collective-permute-start | bytes 138248 | tf_op jit(solution)/shard_map/ppermute | solution.py:17
  21.4 1.0 collective-permute-start.3
  22.4 3.3 %collective-permute-done.2 = f32[10,1,64,18]{2,1,0,3:T(1,128)S(1)} collective-permute-done((f32[10,1,64,18]{2,1,0,3:T(1,128)S(1)}, f32[10,1,64,18]{2,1,0,3:T(1,128)S(1)}, u32[]{:S(2)}, u32[]{:S(2)}) %collective-permute-start.2) | collective-permute-done | bytes 46112 | tf_op jit(solution)/shard_map/ppermute | solution.py:17
  25.7 2.5 %collective-permute-done.3 = f32[10,1,64,18]{2,1,0,3:T(1,128)S(1)} collective-permute-done((f32[10,1,64,18]{2,1,0,3:T(1,128)S(1)}, f32[10,1,64,18]{2,1,0,3:T(1,128)S(1)}, u32[]{:S(2)}, u32[]{:S(2)}) %collective-permute-start.3) | collective-permute-done | bytes 46112 | tf_op jit(solution)/shard_map/ppermute | solution.py:19
  28.2 3.1 %fusion.7 = (f32[8,16,64]{2,1,0:T(8,128)}, f32[8,16,64,18]{2,1,0,3:T(8,128)S(1)}) fusion(f32[10,1,64,18]{2,1,0,3:T(1,128)S(1)} %collective-permute-done.3, f32[10,16,64,18]{2,1,0,3:T(8,128)S(1)} %constant_dynamic-update-slice_fusion, f32[1,16,64,18]{2,1,0,3:T(8,128)S(1)} %collective-permute-done.1, f32[8,16,64,18]{2,1,0,3:T(8,128)S(1)} %reshape.34, ...), kind=kLoop, calls=%fused_computation.24 | loop fusion | flops 3383296 | bytes 2189312 | tf_op jit(solution)/shard_map/reduce_sum | solution.py:55
  31.4 0.3 fusion.5
  31.7 0.1 collective-permute-start.4
  31.8 1.7 collective-permute-start.5
  33.5 2.8 %collective-permute-done.4 = f32[1,16,64,18]{2,1,0,3:T(8,128)S(1)} collective-permute-done((f32[1,16,64,18]{2,1,0,3:T(8,128)S(1)}, f32[1,16,64,18]{2,1,0,3:T(8,128)S(1)}, u32[]{:S(2)}, u32[]{:S(2)}) %collective-permute-start.4) | collective-permute-done | bytes 73760 | tf_op jit(solution)/shard_map/ppermute | solution.py:17
  36.3 0.7 collective-permute-done.5
  37.0 0.2 pad_maximum_fusion.11
  37.2 1.6 collective-permute-start.6
  38.8 1.4 collective-permute-start.7
  40.2 4.6 %convolution_multiply_fusion.2 = f32[18,512]{1,0:T(8,128)S(1)} fusion(bf16[8192,512]{1,0:T(8,128)(2,1)} %bitcast.24, f32[8192,18]{0,1:T(8,128)S(1)} %get-tuple-element.29), kind=kOutput, calls=%fused_computation.55 | convolution fusion | flops 151446528 | bytes 9015296 | tf_op jit(solution)/shard_map/dot_general | solution.py:70
  44.7 0.0 collective-permute-done.6
  44.8 0.0 collective-permute-done.7
  44.8 0.4 maximum_maximum_fusion
  45.2 0.7 fusion.21
  45.9 0.0 copy-start.1
  45.9 0.4 reshape.35
  46.3 0.3 copy-done.1
  46.7 5.8 %multiply_convert_fusion = (bf16[8192,18]{0,1:T(8,128)(2,1)S(1)}, f32[18]{0:T(128)S(1)}, bf16[8192,18]{0,1:T(8,128)(2,1)S(1)}, f32[8192,18]{0,1:T(8,128)S(1)}) fusion(f32[8192,18]{0,1:T(8,128)S(1)} %reshape.35, f32[8192,18]{0,1:T(8,128)S(1)} %get-tuple-element.29, bf16[8192,512]{1,0:T(8,128)(2,1)} %bitcast.25, bf16[18,512]{1,0:T(8,128)(2,1)S(1)} %copy-done.1), kind=kOutput, calls=%fused_computation.57 | convolution fusion | flops 152616944 | bytes 10766408 | tf_op jit(solution)/shard_map/dot_general | solution.py:57
  52.5 0.3 convert_reduce_fusion
  52.7 5.3 %fusion.25 = f32[512,36]{0,1:T(8,128)} fusion(bf16[8192,512]{1,0:T(8,128)(2,1)} %bitcast.27, bf16[8192,18]{0,1:T(8,128)(2,1)S(1)} %get-tuple-element.23, bf16[8192,18]{0,1:T(8,128)(2,1)S(1)} %get-tuple-element.21), kind=kOutput, calls=%fused_computation.54 | convolution fusion | flops 303187968 | bytes 9052160 | tf_op jit(solution)/shard_map/dot_general | solution.py:63
  58.0 0.0 all-reduce.3.cloned.1.call-update
  58.1 42.2 %all-reduce = (f32[18]{0:T(128)S(1)}, f32[36]{0:T(128)S(1)}, f32[18,512]{1,0:T(8,128)}) all-reduce(f32[18]{0:T(128)S(1)} %broadcast_multiply_fusion.3, f32[36]{0:T(128)S(1)} %broadcast_multiply_fusion, f32[18,512]{1,0:T(8,128)S(1)} %convolution_multiply_fusion.2), channel_id=1, replica_groups=mesh['ha'=8,'wa'=4] {'ha','wa'}, use_global_device_ids=true, to_apply=%region_1.0 | all-reduce | flops 9270 | bytes 74160 | tf_op jit(solution)/shard_map/psum | solution.py:51
  100.2 0.0 copy-start.2
  100.2 0.6 multiply_subtract_fusion
  100.8 5.9 %convolution_convert_fusion = bf16[8192,512]{1,0:T(8,128)(2,1)} fusion(bf16[512,18]{0,1:T(8,128)(2,1)S(1)} %copy-done, f32[8192,18]{0,1:T(8,128)S(1)} %get-tuple-element.30, f32[8192,18]{0,1:T(8,128)S(1)} %reshape.35, f32[8192,18]{0,1:T(8,128)S(1)} %get-tuple-element.29, f32[18]{0:T(128)S(1)} %get-tuple-element.27), kind=kOutput, calls=%fused_computation | convolution fusion | flops 156221440 | bytes 10176584 | tf_op jit(solution)/shard_map/dot_general | solution.py:78
  106.7 0.0 copy-done.2
  106.7 76.4 %all-reduce.3.cloned.1.call-done = f32[512,36]{0,1:T(8,128)} async-done(((f32[512,36]{0,1:T(8,128)}), f32[512,36]{0,1:T(8,128)}) %all-reduce.3.cloned.1.call-update) | async-done | bytes 73744 | tf_op jit(solution)/shard_map/psum | solution.py:73
  183.1 1.6 fusion.32
  (7 shorter events, 0.1 us)
Async XLA Ops:
  7.2 0.7 copy-start
  7.2 176.0 %all-reduce.3.cloned.1.call-start = ((), (), s32[]{:S(2)}) async-start(), calls=%async_computation | async-start | bytes 163840 | tf_op jit(solution)/shard_map/psum | solution.py:73
  13.7 4.6 %collective-permute-start = (f32[1,16,64,18]{2,1,0,3:T(8,128)S(1)}, f32[1,16,64,18]{2,1,0,3:T(8,128)S(1)}, u32[]{:S(2)}, u32[]{:S(2)}) collective-permute-start(f32[1,16,64,18]{2,1,0,3:T(8,128)S(1)} %bitcast.29), channel_id=1, source_target_pairs={{0,4},{4,8},{8,12},{12,16},{16,20},{20,24},{24,28},{28,0},{1,5},{5... | collective-permute-start | bytes 221192 | tf_op jit(solution)/shard_map/ppermute | solution.py:17
  13.9 5.3 %collective-permute-start.1 = (f32[1,16,64,18]{2,1,0,3:T(8,128)S(1)}, f32[1,16,64,18]{2,1,0,3:T(8,128)S(1)}, u32[]{:S(2)}, u32[]{:S(2)}) collective-permute-start(f32[1,16,64,18]{2,1,0,3:T(8,128)S(1)} %bitcast.30), channel_id=1, source_target_pairs={{4,0},{8,4},{12,8},{16,12},{20,16},{24,20},{28,24},{0,28},{5,1},{9... | collective-permute-start | bytes 221192 | tf_op jit(solution)/shard_map/ppermute | solution.py:19
  19.3 6.4 %collective-permute-start.2 = (f32[10,1,64,18]{2,1,0,3:T(1,128)S(1)}, f32[10,1,64,18]{2,1,0,3:T(1,128)S(1)}, u32[]{:S(2)}, u32[]{:S(2)}) collective-permute-start(f32[10,1,64,18]{2,1,0,3:T(1,128)S(1)} %get-tuple-element.17), channel_id=1, source_target_pairs={{0,1},{1,2},{2,3},{3,0},{4,5},{5,6},{6,7},{7,4},{8,9},{9,10},{10,1... | collective-permute-start | bytes 138248 | tf_op jit(solution)/shard_map/ppermute | solution.py:17
  21.4 6.8 %collective-permute-start.3 = (f32[10,1,64,18]{2,1,0,3:T(1,128)S(1)}, f32[10,1,64,18]{2,1,0,3:T(1,128)S(1)}, u32[]{:S(2)}, u32[]{:S(2)}) collective-permute-start(f32[10,1,64,18]{2,1,0,3:T(1,128)S(1)} %get-tuple-element.18), channel_id=1, source_target_pairs={{1,0},{2,1},{3,2},{0,3},{5,4},{6,5},{7,6},{4,7},{9,8},{10,9},{11,1... | collective-permute-start | bytes 138248 | tf_op jit(solution)/shard_map/ppermute | solution.py:19
  31.7 4.6 %collective-permute-start.4 = (f32[1,16,64,18]{2,1,0,3:T(8,128)S(1)}, f32[1,16,64,18]{2,1,0,3:T(8,128)S(1)}, u32[]{:S(2)}, u32[]{:S(2)}) collective-permute-start(f32[1,16,64,18]{2,1,0,3:T(8,128)S(1)} %get-tuple-element.19), channel_id=1, source_target_pairs={{0,4},{4,8},{8,12},{12,16},{16,20},{20,24},{24,28},{28,0},{1,5},{5... | collective-permute-start | bytes 221192 | tf_op jit(solution)/shard_map/ppermute | solution.py:17
  31.8 5.3 %collective-permute-start.5 = (f32[1,16,64,18]{2,1,0,3:T(8,128)S(1)}, f32[1,16,64,18]{2,1,0,3:T(8,128)S(1)}, u32[]{:S(2)}, u32[]{:S(2)}) collective-permute-start(f32[1,16,64,18]{2,1,0,3:T(8,128)S(1)} %get-tuple-element.20), channel_id=1, source_target_pairs={{4,0},{8,4},{12,8},{16,12},{20,16},{24,20},{28,24},{0,28},{5,1},{9... | collective-permute-start | bytes 221192 | tf_op jit(solution)/shard_map/ppermute | solution.py:19
  37.2 7.6 %collective-permute-start.6 = (f32[10,1,64,18]{2,1,0,3:T(1,128)S(1)}, f32[10,1,64,18]{2,1,0,3:T(1,128)S(1)}, u32[]{:S(2)}, u32[]{:S(2)}) collective-permute-start(f32[10,1,64,18]{2,1,0,3:T(1,128)S(1)} %get-tuple-element.15), channel_id=1, source_target_pairs={{0,1},{1,2},{2,3},{3,0},{4,5},{5,6},{6,7},{7,4},{8,9},{9,10},{10,1... | collective-permute-start | bytes 138248 | tf_op jit(solution)/shard_map/ppermute | solution.py:17
  38.8 6.0 %collective-permute-start.7 = (f32[10,1,64,18]{2,1,0,3:T(1,128)S(1)}, f32[10,1,64,18]{2,1,0,3:T(1,128)S(1)}, u32[]{:S(2)}, u32[]{:S(2)}) collective-permute-start(f32[10,1,64,18]{2,1,0,3:T(1,128)S(1)} %get-tuple-element.16), channel_id=1, source_target_pairs={{1,0},{2,1},{3,2},{0,3},{5,4},{6,5},{7,6},{4,7},{9,8},{10,9},{11,1... | collective-permute-start | bytes 138248 | tf_op jit(solution)/shard_map/ppermute | solution.py:19
  45.9 0.7 copy-start.1
  100.2 6.5 %copy-start.2 = (f32[18]{0:T(128)}, f32[18]{0:T(128)S(1)}, u32[]{:S(2)}) copy-start(f32[18]{0:T(128)S(1)} %get-tuple-element.6) | copy-start | bytes 220
Sparse Core Ops, SparseCore 0:
  58.2 124.8 all-reduce.2
where the time goes:
time: 192 us
  waiting for transfers between devices  88.8 us (46%)
  blocking collectives  42.2 us (22%)
  matrix products  27.2 us (14%)
  between operations  14.2 us (7%)
  starting transfers between devices  9.68 us (5%)
  other arithmetic  7.18 us (4%)
  local copies, waits for them, and re-layouts  2.33 us (1%)
    psum x1, waiting for transfers between devices, local(): lax.psum((latent_part, column_part, up_part), ('ha', 'wa'))  76.4 us
    psum x1, blocking collectives, local(): marginal = lax.psum(local_mass, ('ha', 'wa'))  42.2 us
    ppermute x4, waiting for transfers between devices, extended_2(): lax.ppermute(tail, axis, [(i, (i + 1) % count) for i in range(count)])  8.36 us
    ppermute x4, starting transfers between devices, extended_2(): lax.ppermute(head, axis, [((i + 1) % count, i) for i in range(count)])  5.91 us
    dot_general x1, matrix products, local(): jnp.dot(logit_grad, w_down.T, preferred_element_type=jnp.float32)  5.89 us
    dot_general x1, matrix products, local(): code_grad = jnp.dot(outward, w_up.T, preferred_element_type=jnp.float32)  5.8 us
    dot_general x1, matrix products, local(): jnp.dot(flattened, w_down, preferred_element_type=jnp.float32) + bit_bias  5.7 us
    dot_general x1, matrix products, local(): lax.dot_general(flattened, stacked, (((0,), (0,)), ((), ())), preferred_e...  5.3 us
  transfers between devices with their start and end apart: 9, of which 7 were waited for; matrix products, arithmetic and copies ran while one was open for 6% of the time, Pallas kernels for 0%

commit v1 on v0

--- a/solution.py
+++ b/solution.py
@@ -48,7 +48,7 @@
     prob = 0.01 + 0.98 * squash
     wide_prob = extended_2(prob.reshape(rows, cols, images, bits), (("ha", 0), ("wa", 1)), layers)
     local_mass = jnp.sum(prob, axis=0) / count
-    marginal = lax.psum(local_mass, ("ha", "wa"))
+    marginal = lax.psum(lax.psum(local_mass, "wa"), "ha")
     wide_pooled = window(wide_prob, rows + 2 * layers - 2, cols + 2 * layers - 2)
     slope = local_weight * jnp.log((1.0 - wide_pooled) / wide_pooled)
     wide_slope = extended_2(slope, (("ha", 0), ("wa", 1)), 1)

time: 192 us -> 214 us (1.11)
  blocking collectives: 42.2 us -> 64.6 us
    psum x1 -> x3, blocking collectives: 42.2 us -> 64.6 us  [the longest x1 43 us: local(): lax.psum((latent_part, column_part, up_part), ('ha', 'wa'))]
  transfers between devices with their start and end apart: 9 -> 9, of which waited for: 7 -> 7; matrix products, arithmetic and copies ran while one was open for 6% -> 5% of each run, Pallas kernels for 0% -> 0%
where the time goes in v1:
time: 214 us; the launch traced here: 213 us
  waiting for transfers between devices  87.9 us (41%)
  blocking collectives  64.6 us (30%)
  matrix products  27.2 us (13%)
  between operations  14.2 us (7%)
  starting transfers between devices  9.68 us (5%)
  other arithmetic  7.18 us (3%)
  local copies, waits for them, and re-layouts  2.33 us (1%)
    psum x1, waiting for transfers between devices, local(): lax.psum((latent_part, column_part, up_part), ('ha', 'wa'))  75.6 us
    psum x1, blocking collectives, local(): lax.psum((latent_part, column_part, up_part), ('ha', 'wa'))  43 us
    psum x2, blocking collectives, local(): marginal = lax.psum(lax.psum(local_mass, 'wa'), 'ha')  21.6 us
    ppermute x4, waiting for transfers between devices, extended_2(): lax.ppermute(tail, axis, [(i, (i + 1) % count) for i in range(count)])  8.36 us
    ppermute x4, starting transfers between devices, extended_2(): lax.ppermute(head, axis, [((i + 1) % count, i) for i in range(count)])  5.91 us
    dot_general x1, matrix products, local(): jnp.dot(logit_grad, w_down.T, preferred_element_type=jnp.float32)  5.89 us
    dot_general x1, matrix products, local(): code_grad = jnp.dot(outward, w_up.T, preferred_element_type=jnp.float32)  5.8 us
    dot_general x1, matrix products, local(): jnp.dot(flattened, w_down, preferred_element_type=jnp.float32) + bit_bias  5.7 us
  transfers between devices with their start and end apart: 9, of which 7 were waited for; matrix products, arithmetic and copies ran while one was open for 5% of the time, Pallas kernels for 0%

profile of v1, /device:TPU:8, one launch (start us, length us, event | category | flops | bytes accessed | tf_op | source)
XLA Modules:
  0.0 213.1 jit_solution(2443750863799765451)
XLA Ops:
  7.2 0.0 copy-start
  7.2 0.0 all-reduce.3.cloned.1.call-start
  7.2 0.7 copy-done
  7.9 5.7 %multiply_add_fusion = (f32[8192,18]{0,1:T(8,128)S(1)}, f32[8192,18]{0,1:T(8,128)S(1)}) fusion(f32[18]{0:T(128)} %param.8, bf16[8192,512]{1,0:T(8,128)(2,1)} %bitcast.26, bf16[512,18]{0,1:T(8,128)(2,1)S(1)} %copy-done), kind=kOutput, calls=%fused_computation.59 | convolution fusion | flops 151879680 | bytes 9586760 | tf_op jit(solution)/shard_map/dot_general | solution.py:46
  13.6 0.1 slice.107
  13.7 0.0 collective-permute-start
  13.8 0.1 slice.109
  13.9 1.8 collective-permute-start.1
  15.6 0.5 reshape.34
  16.1 2.2 %collective-permute-done = f32[1,16,64,18]{2,1,0,3:T(8,128)S(1)} collective-permute-done((f32[1,16,64,18]{2,1,0,3:T(8,128)S(1)}, f32[1,16,64,18]{2,1,0,3:T(8,128)S(1)}, u32[]{:S(2)}, u32[]{:S(2)}) %collective-permute-start) | collective-permute-done | bytes 73760 | tf_op jit(solution)/shard_map/ppermute | solution.py:17
  18.3 0.1 constant_dynamic-update-slice_fusion.1
  18.4 0.7 collective-permute-done.1
  19.2 0.1 fusion.42
  19.3 2.0 collective-permute-start.2
  21.4 1.0 collective-permute-start.3
  22.4 3.3 %collective-permute-done.2 = f32[10,1,64,18]{2,1,0,3:T(1,128)S(1)} collective-permute-done((f32[10,1,64,18]{2,1,0,3:T(1,128)S(1)}, f32[10,1,64,18]{2,1,0,3:T(1,128)S(1)}, u32[]{:S(2)}, u32[]{:S(2)}) %collective-permute-start.2) | collective-permute-done | bytes 46112 | tf_op jit(solution)/shard_map/ppermute | solution.py:17
  25.7 2.5 %collective-permute-done.3 = f32[10,1,64,18]{2,1,0,3:T(1,128)S(1)} collective-permute-done((f32[10,1,64,18]{2,1,0,3:T(1,128)S(1)}, f32[10,1,64,18]{2,1,0,3:T(1,128)S(1)}, u32[]{:S(2)}, u32[]{:S(2)}) %collective-permute-start.3) | collective-permute-done | bytes 46112 | tf_op jit(solution)/shard_map/ppermute | solution.py:19
  28.2 3.1 %fusion.7 = (f32[8,16,64]{2,1,0:T(8,128)}, f32[8,16,64,18]{2,1,0,3:T(8,128)S(1)}) fusion(f32[10,1,64,18]{2,1,0,3:T(1,128)S(1)} %collective-permute-done.3, f32[10,16,64,18]{2,1,0,3:T(8,128)S(1)} %constant_dynamic-update-slice_fusion, f32[1,16,64,18]{2,1,0,3:T(8,128)S(1)} %collective-permute-done.1, f32[8,16,64,18]{2,1,0,3:T(8,128)S(1)} %reshape.34, ...), kind=kLoop, calls=%fused_computation.24 | loop fusion | flops 3383296 | bytes 2189312 | tf_op jit(solution)/shard_map/reduce_sum | solution.py:55
  31.4 0.3 fusion.5
  31.7 0.1 collective-permute-start.4
  31.8 1.7 collective-permute-start.5
  33.5 2.8 %collective-permute-done.4 = f32[1,16,64,18]{2,1,0,3:T(8,128)S(1)} collective-permute-done((f32[1,16,64,18]{2,1,0,3:T(8,128)S(1)}, f32[1,16,64,18]{2,1,0,3:T(8,128)S(1)}, u32[]{:S(2)}, u32[]{:S(2)}) %collective-permute-start.4) | collective-permute-done | bytes 73760 | tf_op jit(solution)/shard_map/ppermute | solution.py:17
  36.3 0.7 collective-permute-done.5
  37.0 0.2 pad_maximum_fusion.11
  37.2 1.6 collective-permute-start.6
  38.8 1.4 collective-permute-start.7
  40.2 4.6 %convolution_multiply_fusion.2 = f32[18,512]{1,0:T(8,128)S(1)} fusion(bf16[8192,512]{1,0:T(8,128)(2,1)} %bitcast.24, f32[8192,18]{0,1:T(8,128)S(1)} %get-tuple-element.28), kind=kOutput, calls=%fused_computation.55 | convolution fusion | flops 151446528 | bytes 9015296 | tf_op jit(solution)/shard_map/dot_general | solution.py:70
  44.7 0.0 collective-permute-done.6
  44.8 0.0 collective-permute-done.7
  44.8 0.4 maximum_maximum_fusion
  45.2 0.7 fusion.21
  45.9 0.0 copy-start.1
  45.9 0.4 reshape.35
  46.3 0.3 copy-done.1
  46.7 5.8 %fusion.39 = (f32[18]{0:T(128)S(1)}, bf16[8192,18]{0,1:T(8,128)(2,1)S(1)}, bf16[8192,18]{0,1:T(8,128)(2,1)S(1)}, f32[8192,18]{0,1:T(8,128)S(1)}) fusion(f32[8192,18]{0,1:T(8,128)S(1)} %get-tuple-element.28, f32[8192,18]{0,1:T(8,128)S(1)} %reshape.35, bf16[8192,512]{1,0:T(8,128)(2,1)} %bitcast.25, bf16[18,512]{1,0:T(8,128)(2,1)S(1)} %copy-done.1), kind=kOutput, calls=%fused_computation.87 | convolution fusion | flops 152616944 | bytes 10766408 | tf_op jit(solution)/shard_map/dot_general | solution.py:57
  52.5 5.3 %fusion.25 = f32[512,36]{0,1:T(8,128)} fusion(bf16[8192,512]{1,0:T(8,128)(2,1)} %bitcast.27, bf16[8192,18]{0,1:T(8,128)(2,1)S(1)} %get-tuple-element.22, bf16[8192,18]{0,1:T(8,128)(2,1)S(1)} %get-tuple-element.21), kind=kOutput, calls=%fused_computation.54 | convolution fusion | flops 303187968 | bytes 9052160 | tf_op jit(solution)/shard_map/dot_general | solution.py:63
  57.7 0.3 convert_reduce_fusion
  58.0 9.1 %psum.35 = f32[18]{0:T(128)S(1)} all-reduce(f32[18]{0:T(128)S(1)} %broadcast_multiply_fusion.3), channel_id=1, replica_groups=mesh['ha'=8,'wa'=4] {'wa'}, use_global_device_ids=true, to_apply=%region_1.0 | all-reduce | flops 18 | bytes 144 | tf_op jit(solution)/shard_map/psum | solution.py:51
  67.1 12.5 %psum.36 = f32[18]{0:T(128)S(1)} all-reduce(f32[18]{0:T(128)S(1)} %psum.35), channel_id=1, replica_groups=mesh['ha'=8,'wa'=4] {'ha'}, use_global_device_ids=true, to_apply=%region_2.0 | all-reduce | flops 18 | bytes 144 | tf_op jit(solution)/shard_map/psum | solution.py:51
  79.6 0.0 copy-start.2
  79.6 0.0 all-reduce.3.cloned.1.call-update
  79.7 43.0 %all-reduce = (f32[36]{0:T(128)S(1)}, f32[18,512]{1,0:T(8,128)}) all-reduce(f32[36]{0:T(128)S(1)} %broadcast_multiply_fusion, f32[18,512]{1,0:T(8,128)S(1)} %convolution_multiply_fusion.2), channel_id=1, replica_groups=mesh['ha'=8,'wa'=4] {'ha','wa'}, use_global_device_ids=true, to_apply=%region_6.0 | all-reduce | flops 9252 | bytes 74016 | tf_op jit(solution)/shard_map/psum | solution.py:73
  122.7 0.6 multiply_subtract_fusion
  123.2 5.9 %convolution_convert_fusion = bf16[8192,512]{1,0:T(8,128)(2,1)} fusion(bf16[512,18]{0,1:T(8,128)(2,1)S(1)} %copy-done, f32[8192,18]{0,1:T(8,128)S(1)} %get-tuple-element.29, f32[8192,18]{0,1:T(8,128)S(1)} %reshape.35, f32[8192,18]{0,1:T(8,128)S(1)} %get-tuple-element.28, f32[18]{0:T(128)S(1)} %get-tuple-element.26), kind=kOutput, calls=%fused_computation | convolution fusion | flops 156221440 | bytes 10176584 | tf_op jit(solution)/shard_map/dot_general | solution.py:78
  129.1 0.0 copy-done.2
  129.1 75.6 %all-reduce.3.cloned.1.call-done = f32[512,36]{0,1:T(8,128)} async-done(((f32[512,36]{0,1:T(8,128)}), f32[512,36]{0,1:T(8,128)}) %all-reduce.3.cloned.1.call-update) | async-done | bytes 73744 | tf_op jit(solution)/shard_map/psum | solution.py:73
  204.7 1.6 fusion.32
  (7 shorter events, 0.1 us)
Async XLA Ops:
  7.2 0.7 copy-start
  7.2 197.5 %all-reduce.3.cloned.1.call-start = ((), (), s32[]{:S(2)}) async-start(), calls=%async_computation | async-start | bytes 163840 | tf_op jit(solution)/shard_map/psum | solution.py:73
  13.7 4.6 %collective-permute-start = (f32[1,16,64,18]{2,1,0,3:T(8,128)S(1)}, f32[1,16,64,18]{2,1,0,3:T(8,128)S(1)}, u32[]{:S(2)}, u32[]{:S(2)}) collective-permute-start(f32[1,16,64,18]{2,1,0,3:T(8,128)S(1)} %bitcast.29), channel_id=1, source_target_pairs={{0,4},{4,8},{8,12},{12,16},{16,20},{20,24},{24,28},{28,0},{1,5},{5... | collective-permute-start | bytes 221192 | tf_op jit(solution)/shard_map/ppermute | solution.py:17
  13.9 5.3 %collective-permute-start.1 = (f32[1,16,64,18]{2,1,0,3:T(8,128)S(1)}, f32[1,16,64,18]{2,1,0,3:T(8,128)S(1)}, u32[]{:S(2)}, u32[]{:S(2)}) collective-permute-start(f32[1,16,64,18]{2,1,0,3:T(8,128)S(1)} %bitcast.30), channel_id=1, source_target_pairs={{4,0},{8,4},{12,8},{16,12},{20,16},{24,20},{28,24},{0,28},{5,1},{9... | collective-permute-start | bytes 221192 | tf_op jit(solution)/shard_map/ppermute | solution.py:19
  19.3 6.4 %collective-permute-start.2 = (f32[10,1,64,18]{2,1,0,3:T(1,128)S(1)}, f32[10,1,64,18]{2,1,0,3:T(1,128)S(1)}, u32[]{:S(2)}, u32[]{:S(2)}) collective-permute-start(f32[10,1,64,18]{2,1,0,3:T(1,128)S(1)} %get-tuple-element.16), channel_id=1, source_target_pairs={{0,1},{1,2},{2,3},{3,0},{4,5},{5,6},{6,7},{7,4},{8,9},{9,10},{10,1... | collective-permute-start | bytes 138248 | tf_op jit(solution)/shard_map/ppermute | solution.py:17
  21.4 6.8 %collective-permute-start.3 = (f32[10,1,64,18]{2,1,0,3:T(1,128)S(1)}, f32[10,1,64,18]{2,1,0,3:T(1,128)S(1)}, u32[]{:S(2)}, u32[]{:S(2)}) collective-permute-start(f32[10,1,64,18]{2,1,0,3:T(1,128)S(1)} %get-tuple-element.17), channel_id=1, source_target_pairs={{1,0},{2,1},{3,2},{0,3},{5,4},{6,5},{7,6},{4,7},{9,8},{10,9},{11,1... | collective-permute-start | bytes 138248 | tf_op jit(solution)/shard_map/ppermute | solution.py:19
  31.7 4.6 %collective-permute-start.4 = (f32[1,16,64,18]{2,1,0,3:T(8,128)S(1)}, f32[1,16,64,18]{2,1,0,3:T(8,128)S(1)}, u32[]{:S(2)}, u32[]{:S(2)}) collective-permute-start(f32[1,16,64,18]{2,1,0,3:T(8,128)S(1)} %get-tuple-element.18), channel_id=1, source_target_pairs={{0,4},{4,8},{8,12},{12,16},{16,20},{20,24},{24,28},{28,0},{1,5},{5... | collective-permute-start | bytes 221192 | tf_op jit(solution)/shard_map/ppermute | solution.py:17
  31.8 5.3 %collective-permute-start.5 = (f32[1,16,64,18]{2,1,0,3:T(8,128)S(1)}, f32[1,16,64,18]{2,1,0,3:T(8,128)S(1)}, u32[]{:S(2)}, u32[]{:S(2)}) collective-permute-start(f32[1,16,64,18]{2,1,0,3:T(8,128)S(1)} %get-tuple-element.19), channel_id=1, source_target_pairs={{4,0},{8,4},{12,8},{16,12},{20,16},{24,20},{28,24},{0,28},{5,1},{9... | collective-permute-start | bytes 221192 | tf_op jit(solution)/shard_map/ppermute | solution.py:19
  37.2 7.6 %collective-permute-start.6 = (f32[10,1,64,18]{2,1,0,3:T(1,128)S(1)}, f32[10,1,64,18]{2,1,0,3:T(1,128)S(1)}, u32[]{:S(2)}, u32[]{:S(2)}) collective-permute-start(f32[10,1,64,18]{2,1,0,3:T(1,128)S(1)} %get-tuple-element.14), channel_id=1, source_target_pairs={{0,1},{1,2},{2,3},{3,0},{4,5},{5,6},{6,7},{7,4},{8,9},{9,10},{10,1... | collective-permute-start | bytes 138248 | tf_op jit(solution)/shard_map/ppermute | solution.py:17
  38.8 6.0 %collective-permute-start.7 = (f32[10,1,64,18]{2,1,0,3:T(1,128)S(1)}, f32[10,1,64,18]{2,1,0,3:T(1,128)S(1)}, u32[]{:S(2)}, u32[]{:S(2)}) collective-permute-start(f32[10,1,64,18]{2,1,0,3:T(1,128)S(1)} %get-tuple-element.15), channel_id=1, source_target_pairs={{1,0},{2,1},{3,2},{0,3},{5,4},{6,5},{7,6},{4,7},{9,8},{10,9},{11,1... | collective-permute-start | bytes 138248 | tf_op jit(solution)/shard_map/ppermute | solution.py:19
  45.9 0.7 copy-start.1
  79.6 49.5 %copy-start.2 = (f32[18]{0:T(128)}, f32[18]{0:T(128)S(1)}, u32[]{:S(2)}) copy-start(f32[18]{0:T(128)S(1)} %psum.36) | copy-start | bytes 220
Sparse Core Ops, SparseCore 0:
  79.8 124.8 all-reduce.2
